TPU v7x, 32 devices: a whole 2x2x4 slice. The times are simulated.
32 devices in a mesh: seq: 8 (over y, x, core), head: 4 (over z).
Axes of the slice: x: 2, y: 2, z: 4, core: 2. Of those that a mesh axis runs over, the one named last changes fastest.
Arguments:
- tokens: bfloat16 [32, 1024, 768], P('seq', 'head'), may hold values from -6 to 6
- skip_values: bfloat16 [32, 1024, 384], P('seq', 'head'), may hold values from -6 to 6
- segments: int32 [32, 1024], P('seq', 'head'), may hold values from 0 to 3, as said below
- token_mask: int32 [32, 1024], P('seq', 'head'), may hold values 0 or 1
- attn_gain: bfloat16 [768], replicated, may hold values from 0.099609375 to 1.8984375
- attn_shift: bfloat16 [768], replicated, may hold values from -1.75 to 1.75
- w_qkv: bfloat16 [768, 1920], replicated, may hold values from -0.21875 to 0.21875
- q_bias: bfloat16 [768], replicated, may hold values from -3 to 3
- v_bias: bfloat16 [384], replicated, may hold values from -3 to 3
- w_out: bfloat16 [768, 768], replicated, may hold values from -0.875 to 0.875
- out_bias: bfloat16 [768], replicated, may hold values from -1.75 to 1.75
- mlp_gain: bfloat16 [768], replicated, may hold values from 0.099609375 to 1.8984375
- mlp_shift: bfloat16 [768], replicated, may hold values from -1.75 to 1.75
- w_up: bfloat16 [768, 3072], replicated, may hold values from -0.21875 to 0.21875
- up_bias: bfloat16 [3072], replicated, may hold values from -3 to 3
- w_down: bfloat16 [3072, 768], replicated, may hold values from -0.109375 to 0.109375
- down_bias: bfloat16 [768], replicated, may hold values from -1.75 to 1.75
- cotangent: bfloat16 [32, 1024, 768], P('seq', 'head'), may hold values from -6 to 6
Outputs:
- layer_out: bfloat16 [32, 1024, 768], P('seq', 'head')
- grad_tokens: float32 [32, 1024, 768], P('seq', 'head')
- grad_skip_values: float32 [32, 1024, 384], P('seq', 'head')
- grad_attn_gain: float32 [768], replicated
- grad_attn_shift: float32 [768], replicated
- grad_w_qkv: float32 [768, 1920], P('seq')
- grad_q_bias: float32 [768], replicated
- grad_v_bias: float32 [384], replicated
- grad_w_out: float32 [768, 768], P('seq')
- grad_out_bias: float32 [768], replicated
- grad_mlp_gain: float32 [768], replicated
- grad_mlp_shift: float32 [768], replicated
- grad_w_up: float32 [768, 3072], P('seq')
- grad_up_bias: float32 [3072], replicated
- grad_w_down: float32 [3072, 768], P('seq')
- grad_down_bias: float32 [768], replicated
Inputs may be any that keep to these rules, and one draw needn't show every extreme that they name: `segments`: within each row the document numbers start at 0 and never fall; in each aligned group of 4 rows one row is a single document, and every other row holds exactly four documents.
All inputs are finite; a program needn't handle non-finite values. No bound on the sum of `token_mask` on one device may be relied on, other than what follows from the above.
Results may differ from a plain program's by a relative error of at most 0.017.
Values may be sent and summed in bfloat16 or wider, within the bound.
No kernel may reach another device: no remote copies, remote signals or barrier semaphores. Data moves between devices by JAX's collectives and lax.ppermute only.
A program may use at most 320 MiB of HBM per device.

v0:
```python
import jax
import jax.numpy as jnp
from jax import lax
from jax.sharding import PartitionSpec as P

HDIM = 64
QBLOCK = 512
EPSILON = 1e-05
MASKED = -1e30


def layer_norm(inputs, norm_gain, norm_shift):
    center = inputs - jnp.mean(inputs, axis=-1, keepdims=True)
    spread = jnp.mean(center * center, axis=-1, keepdims=True)
    return center * lax.rsqrt(spread + EPSILON) * norm_gain + norm_shift


def gelu_tanh(inputs):
    return jax.nn.gelu(inputs, approximate=True)


def split_pairs(array):
    return array.reshape(array.shape[0], array.shape[1], 2, array.shape[2] // 2)


def block_scores(q_block, k_block, seg_items, mask_items, q_start, k_end, factor):
    raw = jnp.einsum("iqhc,ikhc->ihqk", q_block, k_block, preferred_element_type=jnp.float32)
    q_pos = q_start + jnp.arange(q_block.shape[1])
    k_pos = jnp.arange(k_end)
    causal = k_pos[None, :] <= q_pos[:, None]
    diagonal = k_pos[None, :] == q_pos[:, None]
    same_doc = (
        seg_items[:, q_start : q_start + q_block.shape[1], None] == seg_items[:, None, :k_end]
    )
    allowed = same_doc & causal[None] & ((mask_items[:, None, :k_end] == 1) | diagonal[None])
    return jnp.where(allowed[:, None], raw * factor, MASKED)


def body(
    tokens,
    skip_values,
    segments,
    token_mask,
    attn_gain,
    attn_shift,
    w_qkv,
    q_bias,
    v_bias,
    w_out,
    out_bias,
    mlp_gain,
    mlp_shift,
    w_up,
    up_bias,
    w_down,
    down_bias,
    cotangent,
):
    rows_here, seq_here, width = tokens.shape
    pair_width = 2 * HDIM
    pair_count = width // pair_width
    fresh_pairs = pair_count // 2
    factor = float(HDIM) ** (-0.5)
    tokens_f = tokens.astype(jnp.float32)
    normed_f, first_back = jax.vjp(
        layer_norm, tokens_f, attn_gain.astype(jnp.float32), attn_shift.astype(jnp.float32)
    )
    normed = normed_f.astype(jnp.bfloat16)
    w_pairs = w_qkv.reshape(width, 2 * pair_count + fresh_pairs, pair_width)
    project = jnp.einsum("rsd,dpc->rpsc", normed, w_pairs, preferred_element_type=jnp.float32)
    queries = (
        project[:, :pair_count] + q_bias.astype(jnp.float32).reshape(1, pair_count, 1, pair_width)
    ).astype(jnp.bfloat16)
    key_rows = project[:, pair_count : 2 * pair_count].astype(jnp.bfloat16)
    fresh = (
        project[:, 2 * pair_count :]
        + v_bias.astype(jnp.float32).reshape(1, fresh_pairs, 1, pair_width)
    ).astype(jnp.bfloat16)
    reused = skip_values.reshape(rows_here, seq_here, fresh_pairs, pair_width).transpose(0, 2, 1, 3)
    value_rows = jnp.concatenate([fresh, reused], axis=1)
    flat_shape = (rows_here * pair_count, seq_here, pair_width)
    q_items, k_items, v_items = (
        lax.all_to_all(
            queries.reshape(flat_shape), "head", split_axis=0, concat_axis=1, tiled=True
        ),
        lax.all_to_all(
            key_rows.reshape(flat_shape), "head", split_axis=0, concat_axis=1, tiled=True
        ),
        lax.all_to_all(
            value_rows.reshape(flat_shape), "head", split_axis=0, concat_axis=1, tiled=True
        ),
    )
    seg_rows, mask_rows = (
        lax.all_gather(segments, "head", axis=1, tiled=True),
        lax.all_gather(token_mask, "head", axis=1, tiled=True),
    )
    item_count = q_items.shape[0]
    length = q_items.shape[1]
    item_row = (lax.axis_index("head") * item_count + jnp.arange(item_count)) // pair_count
    picker = (item_row[:, None] == jnp.arange(rows_here)[None, :]).astype(jnp.int32)
    seg_items = jnp.sum(picker[:, :, None] * seg_rows[None], axis=1)
    mask_items = jnp.sum(picker[:, :, None] * mask_rows[None], axis=1)
    q_split = split_pairs(q_items)
    k_split = split_pairs(k_items)
    v_split = split_pairs(v_items)
    block_count = length // QBLOCK
    mixed_blocks = []
    log_sums = []
    for block_id in range(block_count):
        q_start = block_id * QBLOCK
        k_end = q_start + QBLOCK
        scores = block_scores(
            q_split[:, q_start:k_end],
            k_split[:, :k_end],
            seg_items,
            mask_items,
            q_start,
            k_end,
            factor,
        )
        row_max = jnp.max(scores, axis=-1, keepdims=True)
        exp_scores = jnp.exp(scores - row_max)
        row_sum = jnp.sum(exp_scores, axis=-1, keepdims=True)
        soft_probs = (exp_scores / row_sum).astype(jnp.bfloat16)
        mixed = jnp.einsum(
            "ihqk,ikhc->iqhc", soft_probs, v_split[:, :k_end], preferred_element_type=jnp.float32
        )
        mixed_blocks.append(mixed.astype(jnp.bfloat16).reshape(item_count, QBLOCK, pair_width))
        log_sums.append(row_max + jnp.log(row_sum))
    mixed_items = jnp.concatenate(mixed_blocks, axis=1)
    mixed_rows = lax.all_to_all(
        mixed_items, "head", split_axis=1, concat_axis=0, tiled=True
    ).reshape(rows_here, pair_count, seq_here, pair_width)
    w_out_pairs = w_out.reshape(pair_count, pair_width, width)
    attended = jnp.einsum(
        "rpsc,pcd->rsd", mixed_rows, w_out_pairs, preferred_element_type=jnp.float32
    ) + out_bias.astype(jnp.float32)
    middle = tokens_f + attended
    normed_mid, second_back = jax.vjp(
        layer_norm, middle, mlp_gain.astype(jnp.float32), mlp_shift.astype(jnp.float32)
    )
    normed_two = normed_mid.astype(jnp.bfloat16)
    hidden = jnp.einsum(
        "rsd,df->rsf", normed_two, w_up, preferred_element_type=jnp.float32
    ) + up_bias.astype(jnp.float32)
    active_f, gelu_back = jax.vjp(gelu_tanh, hidden)
    active = active_f.astype(jnp.bfloat16)
    result = (
        middle
        + jnp.einsum("rsf,fd->rsd", active, w_down, preferred_element_type=jnp.float32)
        + down_bias.astype(jnp.float32)
    )
    layer_out = result.astype(jnp.bfloat16)
    g_down = jnp.einsum("rsf,rsd->fd", active, cotangent, preferred_element_type=jnp.float32)
    g_down_bias = jnp.sum(cotangent, axis=(0, 1), dtype=jnp.float32)
    d_active = jnp.einsum("rsd,fd->rsf", cotangent, w_down, preferred_element_type=jnp.float32)
    d_hidden = gelu_back(d_active)[0].astype(jnp.bfloat16)
    g_up_bias = jnp.sum(d_hidden, axis=(0, 1), dtype=jnp.float32)
    g_up = jnp.einsum("rsd,rsf->df", normed_two, d_hidden, preferred_element_type=jnp.float32)
    d_normed_two = jnp.einsum("rsf,df->rsd", d_hidden, w_up, preferred_element_type=jnp.float32)
    d_mid_norm, g_mlp_gain, g_mlp_shift = second_back(d_normed_two)
    d_middle = cotangent.astype(jnp.float32) + d_mid_norm
    d_att = d_middle.astype(jnp.bfloat16)
    g_out_bias = jnp.sum(d_att, axis=(0, 1), dtype=jnp.float32)
    g_out = jnp.einsum(
        "rpsc,rsd->pcd", mixed_rows, d_att, preferred_element_type=jnp.float32
    ).reshape(width, width)
    d_mixed = (
        jnp.einsum("rsd,pcd->rpsc", d_att, w_out_pairs, preferred_element_type=jnp.float32)
        .astype(jnp.bfloat16)
        .reshape(flat_shape)
    )
    d_items = lax.all_to_all(d_mixed, "head", split_axis=0, concat_axis=1, tiled=True)
    d_split = split_pairs(d_items)
    dk_total = jnp.zeros((item_count, length, 2, HDIM), jnp.float32)
    dv_total = jnp.zeros((item_count, length, 2, HDIM), jnp.float32)
    dq_blocks = []
    for block_id in range(block_count):
        q_start = block_id * QBLOCK
        k_end = q_start + QBLOCK
        scores = block_scores(
            q_split[:, q_start:k_end],
            k_split[:, :k_end],
            seg_items,
            mask_items,
            q_start,
            k_end,
            factor,
        )
        soft = jnp.exp(scores - log_sums[block_id])
        d_block = d_split[:, q_start:k_end]
        d_probs = jnp.einsum(
            "iqhc,ikhc->ihqk", d_block, v_split[:, :k_end], preferred_element_type=jnp.float32
        )
        delta = jnp.sum(d_probs * soft, axis=-1, keepdims=True)
        d_raw = (soft * (d_probs - delta) * factor).astype(jnp.bfloat16)
        dq_blocks.append(
            jnp.einsum(
                "ihqk,ikhc->iqhc", d_raw, k_split[:, :k_end], preferred_element_type=jnp.float32
            )
        )
        dk_total = dk_total.at[:, :k_end].add(
            jnp.einsum(
                "ihqk,iqhc->ikhc",
                d_raw,
                q_split[:, q_start:k_end],
                preferred_element_type=jnp.float32,
            )
        )
        dv_total = dv_total.at[:, :k_end].add(
            jnp.einsum(
                "ihqk,iqhc->ikhc",
                soft.astype(jnp.bfloat16),
                d_block,
                preferred_element_type=jnp.float32,
            )
        )
    item_shape = (item_count, length, pair_width)
    dq_items = jnp.concatenate(dq_blocks, axis=1).astype(jnp.bfloat16).reshape(item_shape)
    dk_items = dk_total.astype(jnp.bfloat16).reshape(item_shape)
    dv_items = dv_total.astype(jnp.bfloat16).reshape(item_shape)
    dq_rows, dk_rows, dv_rows = (
        lax.all_to_all(dq_items, "head", split_axis=1, concat_axis=0, tiled=True),
        lax.all_to_all(dk_items, "head", split_axis=1, concat_axis=0, tiled=True),
        lax.all_to_all(dv_items, "head", split_axis=1, concat_axis=0, tiled=True),
    )
    row_shape = (rows_here, pair_count, seq_here, pair_width)
    dq_rows = dq_rows.reshape(row_shape)
    dk_rows = dk_rows.reshape(row_shape)
    dv_rows = dv_rows.reshape(row_shape)
    grad_skip = (
        dv_rows[:, fresh_pairs:]
        .transpose(0, 2, 1, 3)
        .reshape(rows_here, seq_here, fresh_pairs * pair_width)
        .astype(jnp.float32)
    )
    d_project = jnp.concatenate([dq_rows, dk_rows, dv_rows[:, :fresh_pairs]], axis=1)
    g_qkv = jnp.einsum(
        "rsd,rpsc->dpc", normed, d_project, preferred_element_type=jnp.float32
    ).reshape(width, -1)
    g_q_bias = jnp.sum(dq_rows, axis=(0, 2), dtype=jnp.float32).reshape(-1)
    g_v_bias = jnp.sum(dv_rows[:, :fresh_pairs], axis=(0, 2), dtype=jnp.float32).reshape(-1)
    d_normed = jnp.einsum("rpsc,dpc->rsd", d_project, w_pairs, preferred_element_type=jnp.float32)
    d_tok_norm, g_attn_gain, g_attn_shift = first_back(d_normed)
    grad_tokens = d_middle + d_tok_norm
    small_sums = lax.psum(
        (
            g_attn_gain,
            g_attn_shift,
            g_q_bias,
            g_v_bias,
            g_out_bias,
            g_mlp_gain,
            g_mlp_shift,
            g_up_bias,
            g_down_bias,
        ),
        ("seq", "head"),
    )
    shards = (
        lax.psum_scatter(g_qkv.astype(jnp.bfloat16), "seq", scatter_dimension=0, tiled=True).astype(
            jnp.float32
        ),
        lax.psum_scatter(g_out.astype(jnp.bfloat16), "seq", scatter_dimension=0, tiled=True).astype(
            jnp.float32
        ),
        lax.psum_scatter(g_up.astype(jnp.bfloat16), "seq", scatter_dimension=0, tiled=True).astype(
            jnp.float32
        ),
        lax.psum_scatter(
            g_down.astype(jnp.bfloat16), "seq", scatter_dimension=0, tiled=True
        ).astype(jnp.float32),
    )
    reduced = (
        lax.psum(shards[0].astype(jnp.bfloat16), "head").astype(jnp.float32),
        lax.psum(shards[1].astype(jnp.bfloat16), "head").astype(jnp.float32),
        lax.psum(shards[2].astype(jnp.bfloat16), "head").astype(jnp.float32),
        lax.psum(shards[3].astype(jnp.bfloat16), "head").astype(jnp.float32),
    )
    return (
        layer_out,
        grad_tokens,
        grad_skip,
        small_sums[0],
        small_sums[1],
        reduced[0],
        small_sums[2],
        small_sums[3],
        reduced[1],
        small_sums[4],
        small_sums[5],
        small_sums[6],
        reduced[2],
        small_sums[7],
        reduced[3],
        small_sums[8],
    )


def solution(mesh):
    return jax.shard_map(
        body,
        mesh=mesh,
        in_specs=(
            P("seq", "head", None),
            P("seq", "head", None),
            P("seq", "head"),
            P("seq", "head"),
            P(),
            P(),
            P(),
            P(),
            P(),
            P(),
            P(),
            P(),
            P(),
            P(),
            P(),
            P(),
            P(),
            P("seq", "head", None),
        ),
        out_specs=(
            P("seq", "head", None),
            P("seq", "head", None),
            P("seq", "head", None),
            P(),
            P(),
            P("seq", None),
            P(),
            P(),
            P("seq", None),
            P(),
            P(),
            P(),
            P("seq", None),
            P(),
            P("seq", None),
            P(),
        ),
        check_vma=False,
    )
```

profile of v0, /device:TPU:0, one launch (start us, length us, event | category | flops | bytes accessed | tf_op | source)
XLA Modules:
  0.0 789.2 jit_solution(16880230888935205155)
XLA Ops:
  14.7 4.7 copy.112
  19.4 5.4 convolution_bitcast_fusion
  24.8 3.0 copy-done.18
  29.3 6.3 all-to-all-start
  35.6 3.4 fusion.94
  39.1 33.6 %all-to-all-done = bf16[24,256,128]{2,1,0:T(8,128)(2,1)} async-done(((bf16[24,256,128]{2,1,0:T(8,128)(2,1)}), bf16[24,256,128]{2,1,0:T(8,128)(2,1)}, u32[]{:S(2)}, u32[]{:S(2)}) %all-to-all-start) | async-done | bytes 1572896 | tf_op jit(solution)/shard_map/all_to_all | solution.py:89
  72.7 4.5 all-to-all-start.1
  77.2 3.3 slice.218
  80.5 38.5 %all_gather.6 = s32[4,1024]{1,0:T(4,128)S(1)} all-gather(s32[4,256]{1,0:T(4,128)S(1)} %copy-done.44), channel_id=1, replica_groups=mesh['seq'=8,'head'=4] {'head'}, dimensions={1}, use_global_device_ids=true | all-gather | bytes 20480 | tf_op jit(solution)/shard_map/all_gather | solution.py:94
  119.0 13.1 %all_gather.7 = s32[4,1024]{1,0:T(4,128)S(1)} all-gather(s32[4,256]{1,0:T(4,128)S(1)} %copy-done.45), channel_id=1, replica_groups=mesh['seq'=8,'head'=4] {'head'}, dimensions={1}, use_global_device_ids=true | all-gather | bytes 20480 | tf_op jit(solution)/shard_map/all_gather | solution.py:95
  132.5 4.5 all-to-all-start.2
  140.7 4.5 or_and_fusion
  145.3 3.8 copy.116
  149.0 3.8 reshape.466
  152.8 3.8 copy.117
  156.6 3.8 reshape.468
  160.4 7.7 all-to-all-done.2
  168.1 3.8 copy.118
  171.8 3.8 reshape.470
  175.6 4.7 fusion.43
  185.1 4.2 fusion.122
  190.8 13.4 %fusion.4 = (f32[6,2,512]{2,1,0:T(2,128)S(1)}, f32[6,2,512,1024]{3,2,1,0:T(8,128)}) fusion(pred[6,512,1024]{2,1,0:T(8,128)(4,1)} %or_and_fusion, bf16[6,1024,2,64]{1,3,2,0:T(8,128)(2,1)} %reshape.470, bf16[6,1024,2,64]{1,3,2,0:T(8,128)(2,1)} %reshape.468), kind=kOutput, calls=%fused_computation.12 | convolution fusion | flops 824174592 | bytes 30695424 | tf_op jit(solution)/shard_map/iqhc,ikhc->ihqk/dot_general | solution.py:27
  204.3 11.9 %fusion.3 = f32[6,2,512]{2,1,0:T(2,128)S(1)} fusion(f32[6,2,512,1024]{3,2,1,0:T(8,128)} %get-tuple-element.165, f32[6,2,512]{2,1,0:T(2,128)S(1)} %get-tuple-element.164, pred[6,512,1024]{2,1,0:T(8,128)(4,1)S(1)} %copy-done.11), kind=kLoop, calls=%fused_computation.9 | loop fusion | flops 25159680 | bytes 28360704 | tf_op jit(solution)/shard_map/reduce_sum | solution.py:123
  216.2 11.5 %fusion.123 = bf16[6,2,64,512]{3,2,1,0:T(8,128)(2,1)S(1)} fusion(bf16[6,1024,2,64]{1,3,2,0:T(8,128)(2,1)S(1)} %copy-done.7, f32[6,2,512,1024]{3,2,1,0:T(8,128)} %get-tuple-element.165, f32[6,2,512]{2,1,0:T(2,128)S(1)} %fusion.3, f32[6,2,512]{2,1,0:T(2,128)S(1)} %get-tuple-element.164, pred[6,512,1024]{2,1,0:T(8,128)(4,1)S(1)} %copy-done.11), kind=kOutput, calls=%fused_computation.135 | convolution fusion | flops 837156864 | bytes 30720000 | tf_op jit(solution)/shard_map/ihqk,ikhc->iqhc/dot_general | solution.py:125
  229.2 3.3 pad_maximum_fusion.1
  232.5 4.6 all-to-all-start.3
  237.3 45.5 %all-to-all-done.3 = bf16[6,1024,128]{2,0,1:T(8,128)(2,1)} async-done(((bf16[6,1024,128]{2,0,1:T(8,128)(2,1)}), bf16[6,1024,128]{2,0,1:T(8,128)(2,1)}, u32[]{:S(2)}, u32[]{:S(2)}) %all-to-all-start.3) | async-done | bytes 1572896 | tf_op jit(solution)/shard_map/all_to_all | solution.py:131
  286.9 8.5 %fusion.79 = f32[4,256,3072]{2,1,0:T(8,128)} fusion(bf16[768,3072]{1,0:T(8,128)(2,1)S(1)} %bitcast.198, f32[4,256,768]{2,1,0:T(8,128)S(1)} %get-tuple-element.169, f32[768]{0:T(1024)S(1)} %convert_element_type.180, f32[768]{0:T(1024)S(1)} %convert_element_type.179, f32[4,256]{1,0:T(4,128)S(1)} %fusion.145, f32[4,256]{1,0:T(4,128)S(1)} %broadcast_multiply_fusion), kind=kOutput, calls=%fused_computation.75 | convolution fusion | flops 4835770368 | bytes 20461568 | tf_op jit(solution)/shard_map/rsd,df->rsf/dot_general | solution.py:143
  295.4 16.8 %convert_reduce_fusion = (f32[3072]{0:T(1024)}, bf16[4,256,3072]{2,1,0:T(8,128)(2,1)}) fusion(f32[4,256,3072]{2,1,0:T(8,128)} %fusion.79, f32[3072]{0:T(1024)S(1)} %convert_element_type.182, bf16[4,256,768]{2,1,0:T(8,128)(2,1)S(1)} %copy-done.15, bf16[3072,768]{1,0:T(8,128)(2,1)S(1)} %bitcast.200), kind=kOutput, calls=%fused_computation.23 | convolution fusion | flops 4904186880 | bytes 25190400 | tf_op jit(solution)/shard_map/rsd,fd->rsf/dot_general | solution.py:156
  312.2 8.5 %multiply_reduce_fusion.2 = (f32[768]{0:T(1024)}, f32[4,256]{1,0:T(4,128)S(1)}, f32[768]{0:T(1024)}, f32[4,256,768]{2,1,0:T(8,128)S(1)}) fusion(f32[4,256,768]{2,1,0:T(8,128)S(1)} %get-tuple-element.169, f32[4,256]{1,0:T(4,128)S(1)} %fusion.145, f32[4,256]{1,0:T(4,128)S(1)} %broadcast_multiply_fusion, f32[768]{0:T(1024)S(1)} %convert_element_type.179, ...), kind=kOutput, calls=%fused_computation.101 | convolution fusion | flops 4838126592 | bytes 17323008 | tf_op jit(solution)/shard_map/rsf,df->rsd/dot_general | solution.py:160
  324.8 4.1 bitcast_convert_fusion.3
  328.9 4.3 convolution_convert_fusion
  333.2 4.4 all-to-all-start.4
  337.6 12.5 %bitcast_convert_fusion = bf16[3072,768]{1,0:T(8,128)(2,1)} fusion(bf16[4,256,768]{2,1,0:T(8,128)(2,1)S(1)} %copy-done.15, f32[4,256,3072]{2,1,0:T(8,128)} %fusion.79, f32[3072]{0:T(1024)S(1)} %convert_element_type.182), kind=kOutput, calls=%fused_computation.45 | convolution fusion | flops 4865654784 | bytes 18886656 | tf_op jit(solution)/shard_map/rsf,rsd->fd/dot_general | solution.py:154
  351.0 23.1 %all-to-all-done.4 = bf16[24,256,128]{2,1,0:T(8,128)(2,1)} async-done(((bf16[24,256,128]{2,1,0:T(8,128)(2,1)}), bf16[24,256,128]{2,1,0:T(8,128)(2,1)}, u32[]{:S(2)}, u32[]{:S(2)}) %all-to-all-start.4) | async-done | bytes 1572896 | tf_op jit(solution)/shard_map/all_to_all | solution.py:173
  374.1 3.9 copy.123
  378.0 3.0 reshape.475
  381.0 8.8 %fusion.110 = f32[6,512,2,64]{1,3,2,0:T(8,128)} fusion(f32[6,2,512,512]{2,3,1,0:T(8,128)} %copy-done.9, f32[6,2,512]{2,1,0:T(2,128)S(1)} %log_add_fusion.1, pred[6,512,512]{1,2,0:T(8,128)(4,1)} %or_and_fusion.1, bf16[6,1024,2,64]{1,3,2,0:T(8,128)(2,1)S(1)} %reshape.475), kind=kOutput, calls=%fused_computation.130 | convolution fusion | flops 415236096 | bytes 16539648 | tf_op jit(solution)/shard_map/ihqk,iqhc->ikhc/dot_general | solution.py:211
  389.8 13.9 %fusion.95 = bf16[6,1024,2,64]{1,3,2,0:T(8,128)(2,1)} fusion(f32[6,512,2,64]{1,3,2,0:T(8,128)} %fusion.110, f32[6,2,512,1024]{3,2,1,0:T(8,128)} %get-tuple-element.165, f32[6,2,512]{2,1,0:T(2,128)S(1)} %log_add_fusion, pred[6,512,1024]{2,1,0:T(8,128)(4,1)S(1)} %copy-done.12, bf16[6,1024,2,64]{1,3,2,0:T(8,128)(2,1)S(1)} %reshape.475), kind=kOutput, calls=%fused_computation.97 | convolution fusion | flops 832045056 | bytes 32268288 | tf_op jit(solution)/shard_map/ihqk,iqhc->ikhc/dot_general | solution.py:211
  403.7 4.0 copy.134
  407.8 4.5 all-to-all-start.7
  412.3 10.9 %bitcast_convert_fusion.1 = bf16[768,3072]{1,0:T(8,128)(2,1)} fusion(bf16[4,256,3072]{2,1,0:T(8,128)(2,1)} %get-tuple-element.173, f32[4,256,768]{2,1,0:T(8,128)} %copy-done.10, f32[768]{0:T(1024)S(1)} %convert_element_type.180, f32[768]{0:T(1024)S(1)} %convert_element_type.179, f32[4,256]{1,0:T(4,128)S(1)} %fusion.145, f32[4,256]{1,0:T(4,128)S(1)} %broadcast_multiply_fusion), kind=kOutput, calls=%fused_computation.46 | convolution fusion | flops 4838129664 | bytes 14170112 | tf_op jit(solution)/shard_map/rsd,rsf->df/dot_general | solution.py:159
  424.6 7.5 fusion.129
  432.1 23.1 %fusion.113 = f32[6,512,2,64]{1,3,2,0:T(8,128)} fusion(f32[6,2,512,512]{2,3,1,0:T(8,128)} %fusion.129, f32[6,2,512,512]{2,3,1,0:T(8,128)} %copy-done.9, f32[6,2,512]{2,1,0:T(2,128)S(1)} %log_add_fusion.1, pred[6,512,512]{1,2,0:T(8,128)(4,1)} %or_and_fusion.1, bf16[6,1024,2,64]{1,3,2,0:T(8,128)(2,1)} %reshape.468), kind=kOutput, calls=%fused_computation.131 | convolution fusion | flops 437262848 | bytes 55885824 | tf_op jit(solution)/shard_map/ihqk,iqhc->ikhc/dot_general | solution.py:203
  455.2 11.5 %fusion.126 = f32[6,2,512,1024]{3,2,1,0:T(8,128)} fusion(bf16[6,1024,2,64]{1,3,2,0:T(8,128)(2,1)S(1)} %copy-done.8, bf16[6,1024,2,64]{1,3,2,0:T(8,128)(2,1)} %copy-done.14), kind=kOutput, calls=%fused_computation.140 | convolution fusion | flops 805306368 | bytes 27525120 | tf_op jit(solution)/shard_map/iqhc,ikhc->ihqk/dot_general | solution.py:192
  466.7 43.3 %fusion.96 = bf16[6,1024,2,64]{1,3,2,0:T(8,128)(2,1)S(1)} fusion(f32[6,512,2,64]{1,3,2,0:T(8,128)} %fusion.113, f32[6,2,512,1024]{3,2,1,0:T(8,128)} %fusion.126, f32[6,2,512,1024]{3,2,1,0:T(8,128)} %get-tuple-element.165, f32[6,2,512]{2,1,0:T(2,128)S(1)} %log_add_fusion, pred[6,512,1024]{2,1,0:T(8,128)(4,1)} %or_and_fusion, ...), kind=kOutput, calls=%fused_computation.99 | convolution fusion | flops 876092416 | bytes 110936064 | tf_op jit(solution)/shard_map/ihqk,iqhc->ikhc/dot_general | solution.py:203
  510.1 3.2 copy.130
  513.3 4.9 all-to-all-start.6
  518.2 20.0 %fusion.116 = bf16[6,2,64,512]{3,2,1,0:T(8,128)(2,1)} fusion(f32[6,2,512,512]{2,3,1,0:T(8,128)} %fusion.129, f32[6,2,512,512]{2,3,1,0:T(8,128)} %copy-done.9, f32[6,2,512]{2,1,0:T(2,128)S(1)} %log_add_fusion.1, pred[6,512,512]{1,2,0:T(8,128)(4,1)} %or_and_fusion.1, bf16[6,1024,2,64]{1,3,2,0:T(8,128)(2,1)} %reshape.470), kind=kOutput, calls=%fused_computation.132 | convolution fusion | flops 437656064 | bytes 55099392 | tf_op jit(solution)/shard_map/ihqk,ikhc->iqhc/dot_general | solution.py:198
  539.9 42.1 %fusion.119 = bf16[6,2,64,512]{3,2,1,0:T(8,128)(2,1)} fusion(bf16[6,1024,2,64]{1,3,2,0:T(8,128)(2,1)} %reshape.470, f32[6,2,512,1024]{3,2,1,0:T(8,128)} %fusion.126, f32[6,2,512,1024]{3,2,1,0:T(8,128)} %get-tuple-element.165, f32[6,2,512]{2,1,0:T(2,128)S(1)} %log_add_fusion, pred[6,512,1024]{2,1,0:T(8,128)(4,1)} %or_and_fusion), kind=kOutput, calls=%fused_computation.133 | convolution fusion | flops 874912768 | bytes 55861248 | tf_op jit(solution)/shard_map/ihqk,ikhc->iqhc/dot_general | solution.py:198
  584.4 3.0 pad_maximum_fusion.2
  587.4 5.1 all-to-all-start.5
  597.4 42.2 %all-to-all-done.5 = bf16[6,1024,128]{2,0,1:T(8,128)(2,1)} async-done(((bf16[6,1024,128]{2,0,1:T(8,128)(2,1)}), bf16[6,1024,128]{2,0,1:T(8,128)(2,1)}, u32[]{:S(2)}, u32[]{:S(2)}) %all-to-all-start.5) | async-done | bytes 1572896 | tf_op jit(solution)/shard_map/all_to_all | solution.py:223
  641.7 7.2 bitcast_convert_fusion.2
  648.8 4.7 copy.140
  653.8 13.5 %add_convert_fusion = bf16[4,256,768]{2,1,0:T(8,128)(2,1)} fusion(f32[4,256,768]{2,1,0:T(8,128)} %copy-done.10, bf16[3072,768]{1,0:T(8,128)(2,1)} %param.45, f32[768]{0:T(1024)S(1)} %convert_element_type.184, f32[4,256,3072]{2,1,0:T(8,128)} %fusion.79, f32[3072]{0:T(1024)S(1)} %convert_element_type.182), kind=kOutput, calls=%fused_computation.106 | convolution fusion | flops 4865654784 | bytes 22035456 | tf_op jit(solution)/shard_map/rsf,fd->rsd/dot_general | solution.py:150
  667.3 30.8 %reduce-scatter.5.cloned.1.call-done = bf16[96,1920]{1,0:T(8,128)(2,1)} async-done(((bf16[768,1920]{1,0:T(8,128)(2,1)}), bf16[96,1920]{1,0:T(8,128)(2,1)}) %reduce-scatter.5.cloned.1.call-update) | async-done | bytes 368656 | tf_op jit(solution)/shard_map/reduce_scatter | solution.py:261
  698.1 7.3 bitcast_reduce_fusion
  705.5 3.3 copy.138
  708.8 3.0 copy.144
  713.2 3.2 fusion.91
  716.5 4.3 convert_reduce_fusion.2
  720.8 41.9 %all-reduce.2 = (f32[768]{0:T(1024)}, f32[768]{0:T(1024)}, f32[768]{0:T(1024)}, f32[384]{0:T(512)}, f32[768]{0:T(1024)}, /*index=5*/f32[768]{0:T(1024)}, f32[768]{0:T(1024)}, f32[3072]{0:T(1024)}, f32[768]{0:T(1024)}) all-reduce(f32[768]{0:T(1024)S(1)} %get-tuple-element.130, ...), channel_id=1, replica_groups=mesh['seq'=8,'head'=4] {'seq','head'}, use_global_device_ids=true, to_apply=%region_17.18 | all-reduce | flops 8832 | bytes 70656 | tf_op jit(solution)/shard_map/psum | solution.py:246
  762.7 12.9 %all-reduce.6.cloned.1.call-done = (bf16[96,1920]{1,0:T(8,128)(2,1)}, bf16[96,768]{1,0:T(8,128)(2,1)}, bf16[96,3072]{1,0:T(8,128)(2,1)}, bf16[384,768]{1,0:T(8,128)(2,1)}) async-done(((bf16[96,1920]{1,0:T(8,128)(2,1)}, bf16[96,768]{1,0:T(8,128)(2,1)}, bf16[96,3072]{1,0:T(8,128)(2,1)}, bf16[384,768]{1,0:T(8,128)(2,1)}), (bf16[96,1920]{1,0:T(8,128)(2,1)}, bf16[96,768]{1,0:T(8,128)(2,1)}, ...) | async-done | bytes 1695760 | tf_op jit(solution)/shard_map/psum | solution.py:275
  (187 shorter events, 50.7 us)
Async XLA Ops:
  7.2 277.4 %copy-start = (bf16[768,768]{1,0:T(8,128)(2,1)S(1)}, bf16[768,768]{1,0:T(8,128)(2,1)}, u32[]{:S(2)}) copy-start(bf16[768,768]{1,0:T(8,128)(2,1)} %param.39) | copy-start | bytes 3538948
  7.2 6.5 copy-start.21
  8.7 10.6 %copy-start.33 = (f32[768]{0:T(1024)}, f32[768]{0:T(1024)S(1)}, u32[]{:S(2)}) copy-start(f32[768]{0:T(1024)S(1)} %convert_element_type.166) | copy-start | bytes 9220
  11.7 7.7 copy-start.31
  13.7 5.6 copy-start.35
  14.7 4.7 copy-start.4
  24.8 3.1 copy-start.18
  28.0 7.6 copy-start.49
  29.3 43.4 %all-to-all-start = ((bf16[24,256,128]{2,1,0:T(8,128)(2,1)}), bf16[24,256,128]{2,1,0:T(8,128)(2,1)}, u32[]{:S(2)}, u32[]{:S(2)}) async-start(bf16[24,256,128]{2,1,0:T(8,128)(2,1)} %bitcast.172), calls=%async_computation | async-start | bytes 3145728 | tf_op jit(solution)/shard_map/all_to_all | solution.py:89
  72.7 7.8 copy-start.44
  72.7 46.3 %copy-start.45 = (s32[4,256]{1,0:T(4,128)S(1)}, s32[4,256]{1,0:T(4,128)}, u32[]{:S(2)}) copy-start(s32[4,256]{1,0:T(4,128)} %param.33) | copy-start | bytes 12292
  72.7 59.8 %all-to-all-start.1 = ((bf16[24,256,128]{2,1,0:T(8,128)(2,1)}), bf16[24,256,128]{2,1,0:T(8,128)(2,1)}, u32[]{:S(2)}, u32[]{:S(2)}) async-start(bf16[24,256,128]{2,1,0:T(8,128)(2,1)} %bitcast.178), calls=%async_computation.1 | async-start | bytes 3145728 | tf_op jit(solution)/shard_map/all_to_all | solution.py:83
  132.5 35.6 %all-to-all-start.2 = ((bf16[24,256,128]{2,1,0:T(8,128)(2,1)}), bf16[24,256,128]{2,1,0:T(8,128)(2,1)}, u32[]{:S(2)}, u32[]{:S(2)}) async-start(bf16[24,256,128]{2,1,0:T(8,128)(2,1)} %bitcast.171), calls=%async_computation.2 | async-start | bytes 3145728 | tf_op jit(solution)/shard_map/all_to_all | solution.py:86
  175.6 4.8 copy-start.17
  180.4 4.7 copy-start.9
  180.4 4.7 copy-start.23
  180.4 4.7 copy-start.6
  185.1 4.2 copy-start.25
  190.8 13.5 %copy-start.11 = (pred[6,512,1024]{2,1,0:T(8,128)(4,1)S(1)}, pred[6,512,1024]{2,1,0:T(8,128)(4,1)}, u32[]{:S(2)}) copy-start(pred[6,512,1024]{2,1,0:T(8,128)(4,1)} %or_and_fusion) | copy-start | bytes 9437188
  204.3 11.9 %copy-start.27 = (f32[6,2,512]{2,1,0:T(2,128)}, f32[6,2,512]{2,1,0:T(2,128)S(1)}, u32[]{:S(2)}) copy-start(f32[6,2,512]{2,1,0:T(2,128)S(1)} %get-tuple-element.164) | copy-start | bytes 73732
  204.3 11.9 %copy-start.7 = (bf16[6,1024,2,64]{1,3,2,0:T(8,128)(2,1)S(1)}, bf16[6,1024,2,64]{1,3,2,0:T(8,128)(2,1)}, u32[]{:S(2)}) copy-start(bf16[6,1024,2,64]{1,3,2,0:T(8,128)(2,1)} %reshape.466) | copy-start | bytes 4718596
  216.2 11.5 %copy-start.29 = (f32[6,2,512]{2,1,0:T(2,128)}, f32[6,2,512]{2,1,0:T(2,128)S(1)}, u32[]{:S(2)}) copy-start(f32[6,2,512]{2,1,0:T(2,128)S(1)} %fusion.3) | copy-start | bytes 73732
  232.5 4.7 copy-start.50
  232.5 4.7 copy-start.51
  232.5 4.7 copy-start.52
  232.5 4.7 copy-start.43
  232.5 50.2 %all-to-all-start.3 = ((bf16[6,1024,128]{2,0,1:T(8,128)(2,1)}), bf16[6,1024,128]{2,0,1:T(8,128)(2,1)}, u32[]{:S(2)}, u32[]{:S(2)}) async-start(bf16[6,1024,128]{2,0,1:T(8,128)(2,1)} %pad_maximum_fusion.1), calls=%async_computation.3 | async-start | bytes 4194304 | tf_op jit(solution)/shard_map/all_to_all | solution.py:131
  237.1 430.2 %reduce-scatter.7.cloned.1.call-start = ((), (), s32[]{:S(2)}) async-start(), calls=%async_computation.13 | async-start | bytes 1327104 | tf_op jit(solution)/shard_map/reduce_scatter | solution.py:264
  284.6 2.2 slice-start
  284.6 2.3 slice-start.1
  284.6 10.8 %slice-start.2 = ((s8[4718592]{0:T(1024)(128)(4,1)}), s8[4194304]{0:T(1024)(128)(4,1)S(1)}, s32[]{:S(2)}) async-start(s8[4718592]{0:T(1024)(128)(4,1)} %bitcast.199), calls=%async_computation.19 | async-start | bytes 8388608
  286.2 34.6 %copy-start.10 = (f32[4,256,768]{2,1,0:T(8,128)}, f32[4,256,768]{2,1,0:T(8,128)S(1)}, u32[]{:S(2)}) copy-start(f32[4,256,768]{2,1,0:T(8,128)S(1)} %get-tuple-element.169) | copy-start | bytes 9437188
  286.9 8.5 %copy-start.15 = (bf16[4,256,768]{2,1,0:T(8,128)(2,1)S(1)}, bf16[4,256,768]{2,1,0:T(8,128)(2,1)}, u32[]{:S(2)}) copy-start(bf16[4,256,768]{2,1,0:T(8,128)(2,1)} %param.47) | copy-start | bytes 4718596
  286.9 8.5 %slice-start.3 = ((s8[4718592]{0:T(1024)(128)(4,1)}), s8[524288]{0:T(1024)(128)(4,1)S(1)}, s32[]{:S(2)}) async-start(s8[4718592]{0:T(1024)(128)(4,1)} %bitcast.199), calls=%async_computation.20 | async-start | bytes 1048576
  322.0 1.6 copy-start.2
  322.0 1.6 copy-start.37
  333.2 40.9 %all-to-all-start.4 = ((bf16[24,256,128]{2,1,0:T(8,128)(2,1)}), bf16[24,256,128]{2,1,0:T(8,128)(2,1)}, u32[]{:S(2)}, u32[]{:S(2)}) async-start(bf16[24,256,128]{2,1,0:T(8,128)(2,1)} %bitcast.189), calls=%async_computation.4 | async-start | bytes 3145728 | tf_op jit(solution)/shard_map/all_to_all | solution.py:173
  337.6 329.7 %reduce-scatter.11.cloned.1.call-start = ((), (), s32[]{:S(2)}) async-start(), calls=%async_computation.15 | async-start | bytes 5308416 | tf_op jit(solution)/shard_map/reduce_scatter | solution.py:270
  381.0 8.8 %copy-start.14 = (bf16[6,1024,2,64]{1,3,2,0:T(8,128)(2,1)}, bf16[6,1024,2,64]{1,3,2,0:T(8,128)(2,1)S(1)}, u32[]{:S(2)}) copy-start(bf16[6,1024,2,64]{1,3,2,0:T(8,128)(2,1)S(1)} %reshape.475) | copy-start | bytes 4718596
  381.0 8.8 %copy-start.12 = (pred[6,512,1024]{2,1,0:T(8,128)(4,1)S(1)}, pred[6,512,1024]{2,1,0:T(8,128)(4,1)}, u32[]{:S(2)}) copy-start(pred[6,512,1024]{2,1,0:T(8,128)(4,1)} %or_and_fusion) | copy-start | bytes 9437188
  407.8 105.6 %all-to-all-start.7 = ((bf16[6,1024,128]{2,0,1:T(8,128)(2,1)}), bf16[6,1024,128]{2,0,1:T(8,128)(2,1)}, u32[]{:S(2)}, u32[]{:S(2)}) async-start(bf16[6,1024,128]{2,0,1:T(8,128)(2,1)} %copy.134), calls=%async_computation.7 | async-start | bytes 4194304 | tf_op jit(solution)/shard_map/all_to_all | solution.py:225
  412.2 255.1 %reduce-scatter.9.cloned.1.call-start = ((), (), s32[]{:S(2)}) async-start(), calls=%async_computation.14 | async-start | bytes 5308416 | tf_op jit(solution)/shard_map/reduce_scatter | solution.py:267
  513.3 74.1 %all-to-all-start.6 = ((bf16[6,1024,128]{2,0,1:T(8,128)(2,1)}), bf16[6,1024,128]{2,0,1:T(8,128)(2,1)S(1)}, u32[]{:S(2)}, u32[]{:S(2)}) async-start(bf16[6,1024,128]{2,0,1:T(8,128)(2,1)} %copy.130), calls=%async_computation.6 | async-start | bytes 4194304 | tf_op jit(solution)/shard_map/all_to_all | solution.py:224
  587.4 52.2 %all-to-all-start.5 = ((bf16[6,1024,128]{2,0,1:T(8,128)(2,1)}), bf16[6,1024,128]{2,0,1:T(8,128)(2,1)}, u32[]{:S(2)}, u32[]{:S(2)}) async-start(bf16[6,1024,128]{2,0,1:T(8,128)(2,1)} %pad_maximum_fusion.2), calls=%async_computation.5 | async-start | bytes 4194304 | tf_op jit(solution)/shard_map/all_to_all | solution.py:223
  592.5 105.6 %reduce-scatter.5.cloned.1.call-start = ((), (), s32[]{:S(2)}) async-start(), calls=%async_computation.12 | async-start | bytes 3317760 | tf_op jit(solution)/shard_map/reduce_scatter | solution.py:261
  594.4 1.7 copy-start.13
  596.1 45.6 %copy-start.5 = (bf16[4,256,768]{2,1,0:T(8,128)(2,1)S(1)}, bf16[4,256,768]{2,1,0:T(8,128)(2,1)}, u32[]{:S(2)}) copy-start(bf16[4,256,768]{2,1,0:T(8,128)(2,1)} %param.30) | copy-start | bytes 4718596
  596.1 45.6 %copy-start.32 = (f32[4,256]{1,0:T(4,128)S(1)}, f32[4,256]{1,0:T(4,128)}, u32[]{:S(2)}) copy-start(f32[4,256]{1,0:T(4,128)} %copy-done.31) | copy-start | bytes 12292
  596.1 45.6 %copy-start.34 = (f32[768]{0:T(1024)S(1)}, f32[768]{0:T(1024)}, u32[]{:S(2)}) copy-start(f32[768]{0:T(1024)} %copy-done.33) | copy-start | bytes 9220
  596.1 45.6 %copy-start.36 = (f32[4,256]{1,0:T(4,128)S(1)}, f32[4,256]{1,0:T(4,128)}, u32[]{:S(2)}) copy-start(f32[4,256]{1,0:T(4,128)} %copy-done.35) | copy-start | bytes 12292
  596.1 45.6 %copy-start.46 = (f32[768]{0:T(1024)S(1)}, f32[768]{0:T(1024)}, u32[]{:S(2)}) copy-start(f32[768]{0:T(1024)} %convert_element_type.167) | copy-start | bytes 9220
  641.6 7.2 copy-start.19
  648.8 4.9 copy-start.53
  653.5 122.1 %all-reduce.6.cloned.1.call-start = ((), (), s32[]{:S(2)}) async-start(), calls=%async_computation.16 | async-start | bytes 3391488 | tf_op jit(solution)/shard_map/psum | solution.py:275
  705.5 7.7 copy-start.40
  711.8 4.7 copy-start.3
  711.8 4.7 copy-start.16
  711.8 4.7 copy-start.38
  716.5 4.3 copy-start.41
  716.5 4.3 copy-start.42
  716.5 4.3 copy-start.47
  716.5 4.3 copy-start.48
  716.5 66.0 %copy-start.1 = (bf16[768,768]{1,0:T(8,128)(2,1)S(1)}, bf16[768,768]{1,0:T(8,128)(2,1)}, u32[]{:S(2)}) copy-start(bf16[768,768]{1,0:T(8,128)(2,1)} %param.39) | copy-start | bytes 3538948
  775.6 5.8 copy-start.22
  (7 other events, 6.2 us)
Sparse Core Ops, SparseCore 0:
  329.0 35.8 reduce-scatter.6
  368.8 53.8 reduce-scatter.10
  426.1 53.8 reduce-scatter.8
  653.7 44.4 reduce-scatter.4
  700.8 74.7 all-reduce.5
where the time goes:
time: 797 us; the launch traced here: 789 us
  matrix products  305 us (38%)
  waiting for transfers between devices  196 us (25%)
  blocking collectives  93.5 us (12%)
  local copies, waits for them, and re-layouts  77.6 us (10%)
  other arithmetic  63.5 us (8%)
  starting transfers between devices  39.1 us (5%)
  between operations  14.8 us (2%)
    dot_general x2, matrix products, body(): jnp.einsum('ihqk,iqhc->ikhc', d_raw, q_split[:, q_start:k_end], preferred...  66.5 us
    dot_general x2, matrix products, body(): jnp.einsum('ihqk,ikhc->iqhc', d_raw, k_split[:, :k_end], preferred_elemen...  62.1 us
    all_to_all x1, waiting for transfers between devices, body(): lax.all_to_all(mixed_items, 'head', split_axis=1, concat_axis=0, tiled=True)  45.5 us
    all_to_all x1, waiting for transfers between devices, body(): lax.all_to_all(dq_items, 'head', split_axis=1, concat_axis=0, tiled=True)  42.2 us
    psum x1, blocking collectives, body(): lax.psum((g_attn_gain, g_attn_shift, g_q_bias, g_v_bias, g_out_bias, g_ml...  41.9 us
    all_gather x1, blocking collectives, body(): lax.all_gather(segments, 'head', axis=1, tiled=True)  38.5 us
    all_to_all x1, waiting for transfers between devices, body(): lax.all_to_all(value_rows.reshape(flat_shape), 'head', split_axis=0, conc...  33.6 us
    reduce_scatter x1, waiting for transfers between devices, body(): lax.psum_scatter(g_qkv.astype(jnp.bfloat16), 'seq', scatter_dimension=0,...  30.8 us
  transfers between devices with their start and end apart: 13, of which 7 were waited for; matrix products, arithmetic and copies ran while one was open for 39% of the time, Pallas kernels for 0%

commit v1 on v0

--- a/solution.py
+++ b/solution.py
@@ -244,18 +244,21 @@
     d_tok_norm, g_attn_gain, g_attn_shift = first_back(d_normed)
     grad_tokens = d_middle + d_tok_norm
     small_sums = lax.psum(
-        (
-            g_attn_gain,
-            g_attn_shift,
-            g_q_bias,
-            g_v_bias,
-            g_out_bias,
-            g_mlp_gain,
-            g_mlp_shift,
-            g_up_bias,
-            g_down_bias,
-        ),
-        ("seq", "head"),
+        lax.psum(
+            (
+                g_attn_gain,
+                g_attn_shift,
+                g_q_bias,
+                g_v_bias,
+                g_out_bias,
+                g_mlp_gain,
+                g_mlp_shift,
+                g_up_bias,
+                g_down_bias,
+            ),
+            "head",
+        ),
+        "seq",
     )
     shards = (
         lax.psum_scatter(g_qkv.astype(jnp.bfloat16), "seq", scatter_dimension=0, tiled=True).astype(

time: 797 us -> 798 us (level)
    psum x0 -> x1, blocking collectives: none -> 24.5 us  [body(): lax.psum(lax.psum((g_attn_gain, g_attn_shift, g_q_bias, g_v_bias, g_out_b...]
    psum x1, blocking collectives: 41.9 us -> 20.5 us  [body(): lax.psum((g_attn_gain, g_attn_shift, g_q_bias, g_v_bias, g_out_bias, g_ml...]
where the time goes in v1:
time: 798 us; the launch traced here: 790 us
  matrix products  305 us (38%)
  waiting for transfers between devices  194 us (24%)
  blocking collectives  96.7 us (12%)
  local copies, waits for them, and re-layouts  77.6 us (10%)
  other arithmetic  63.5 us (8%)
  starting transfers between devices  39.1 us (5%)
  between operations  14.8 us (2%)
    dot_general x2, matrix products, body(): jnp.einsum('ihqk,iqhc->ikhc', d_raw, q_split[:, q_start:k_end], preferred...  66.5 us
    dot_general x2, matrix products, body(): jnp.einsum('ihqk,ikhc->iqhc', d_raw, k_split[:, :k_end], preferred_elemen...  62.2 us
    all_to_all x1, waiting for transfers between devices, body(): lax.all_to_all(mixed_items, 'head', split_axis=1, concat_axis=0, tiled=True)  45.5 us
    all_to_all x1, waiting for transfers between devices, body(): lax.all_to_all(dq_items, 'head', split_axis=1, concat_axis=0, tiled=True)  42.2 us
    all_gather x1, blocking collectives, body(): lax.all_gather(segments, 'head', axis=1, tiled=True)  38.5 us
    all_to_all x1, waiting for transfers between devices, body(): lax.all_to_all(value_rows.reshape(flat_shape), 'head', split_axis=0, conc...  33.6 us
    reduce_scatter x1, waiting for transfers between devices, body(): lax.psum_scatter(g_qkv.astype(jnp.bfloat16), 'seq', scatter_dimension=0,...  30.8 us
    psum x1, blocking collectives, body(): lax.psum(lax.psum((g_attn_gain, g_attn_shift, g_q_bias, g_v_bias, g_out_b...  24.5 us
  transfers between devices with their start and end apart: 13, of which 7 were waited for; matrix products, arithmetic and copies ran while one was open for 39% of the time, Pallas kernels for 0%

profile of v1, /device:TPU:0, one launch (start us, length us, event | category | flops | bytes accessed | tf_op | source)
XLA Modules:
  0.0 790.3 jit_solution(16378577426024484045)
XLA Ops:
  14.7 4.7 copy.112
  19.4 5.4 convolution_bitcast_fusion
  24.8 3.1 copy-done.18
  29.3 6.3 all-to-all-start
  35.6 3.4 fusion.94
  39.1 33.6 %all-to-all-done = bf16[24,256,128]{2,1,0:T(8,128)(2,1)} async-done(((bf16[24,256,128]{2,1,0:T(8,128)(2,1)}), bf16[24,256,128]{2,1,0:T(8,128)(2,1)}, u32[]{:S(2)}, u32[]{:S(2)}) %all-to-all-start) | async-done | bytes 1572896 | tf_op jit(solution)/shard_map/all_to_all | solution.py:89
  72.7 4.5 all-to-all-start.1
  77.2 3.3 slice.218
  80.5 38.5 %all_gather.6 = s32[4,1024]{1,0:T(4,128)S(1)} all-gather(s32[4,256]{1,0:T(4,128)S(1)} %copy-done.44), channel_id=1, replica_groups=mesh['seq'=8,'head'=4] {'head'}, dimensions={1}, use_global_device_ids=true | all-gather | bytes 20480 | tf_op jit(solution)/shard_map/all_gather | solution.py:94
  119.0 13.1 %all_gather.7 = s32[4,1024]{1,0:T(4,128)S(1)} all-gather(s32[4,256]{1,0:T(4,128)S(1)} %copy-done.45), channel_id=1, replica_groups=mesh['seq'=8,'head'=4] {'head'}, dimensions={1}, use_global_device_ids=true | all-gather | bytes 20480 | tf_op jit(solution)/shard_map/all_gather | solution.py:95
  132.5 4.5 all-to-all-start.2
  140.7 4.5 or_and_fusion
  145.3 3.8 copy.116
  149.0 3.8 reshape.466
  152.8 3.8 copy.117
  156.6 3.8 reshape.468
  160.4 7.7 all-to-all-done.2
  168.1 3.8 copy.118
  171.8 3.8 reshape.470
  175.6 4.7 fusion.43
  185.1 4.2 fusion.122
  190.8 13.4 %fusion.4 = (f32[6,2,512]{2,1,0:T(2,128)S(1)}, f32[6,2,512,1024]{3,2,1,0:T(8,128)}) fusion(pred[6,512,1024]{2,1,0:T(8,128)(4,1)} %or_and_fusion, bf16[6,1024,2,64]{1,3,2,0:T(8,128)(2,1)} %reshape.470, bf16[6,1024,2,64]{1,3,2,0:T(8,128)(2,1)} %reshape.468), kind=kOutput, calls=%fused_computation.12 | convolution fusion | flops 824174592 | bytes 30695424 | tf_op jit(solution)/shard_map/iqhc,ikhc->ihqk/dot_general | solution.py:27
  204.3 11.9 %fusion.3 = f32[6,2,512]{2,1,0:T(2,128)S(1)} fusion(f32[6,2,512,1024]{3,2,1,0:T(8,128)} %get-tuple-element.174, f32[6,2,512]{2,1,0:T(2,128)S(1)} %get-tuple-element.173, pred[6,512,1024]{2,1,0:T(8,128)(4,1)S(1)} %copy-done.11), kind=kLoop, calls=%fused_computation.9 | loop fusion | flops 25159680 | bytes 28360704 | tf_op jit(solution)/shard_map/reduce_sum | solution.py:123
  216.2 11.5 %fusion.123 = bf16[6,2,64,512]{3,2,1,0:T(8,128)(2,1)S(1)} fusion(bf16[6,1024,2,64]{1,3,2,0:T(8,128)(2,1)S(1)} %copy-done.7, f32[6,2,512,1024]{3,2,1,0:T(8,128)} %get-tuple-element.174, f32[6,2,512]{2,1,0:T(2,128)S(1)} %fusion.3, f32[6,2,512]{2,1,0:T(2,128)S(1)} %get-tuple-element.173, pred[6,512,1024]{2,1,0:T(8,128)(4,1)S(1)} %copy-done.11), kind=kOutput, calls=%fused_computation.135 | convolution fusion | flops 837156864 | bytes 30720000 | tf_op jit(solution)/shard_map/ihqk,ikhc->iqhc/dot_general | solution.py:125
  229.2 3.3 pad_maximum_fusion.1
  232.5 4.6 all-to-all-start.3
  237.3 45.5 %all-to-all-done.3 = bf16[6,1024,128]{2,0,1:T(8,128)(2,1)} async-done(((bf16[6,1024,128]{2,0,1:T(8,128)(2,1)}), bf16[6,1024,128]{2,0,1:T(8,128)(2,1)}, u32[]{:S(2)}, u32[]{:S(2)}) %all-to-all-start.3) | async-done | bytes 1572896 | tf_op jit(solution)/shard_map/all_to_all | solution.py:131
  286.9 8.5 %fusion.79 = f32[4,256,3072]{2,1,0:T(8,128)} fusion(bf16[768,3072]{1,0:T(8,128)(2,1)S(1)} %bitcast.198, f32[4,256,768]{2,1,0:T(8,128)S(1)} %get-tuple-element.178, f32[768]{0:T(1024)S(1)} %convert_element_type.180, f32[768]{0:T(1024)S(1)} %convert_element_type.179, f32[4,256]{1,0:T(4,128)S(1)} %fusion.145, f32[4,256]{1,0:T(4,128)S(1)} %broadcast_multiply_fusion), kind=kOutput, calls=%fused_computation.75 | convolution fusion | flops 4835770368 | bytes 20461568 | tf_op jit(solution)/shard_map/rsd,df->rsf/dot_general | solution.py:143
  295.4 16.8 %convert_reduce_fusion = (f32[3072]{0:T(1024)}, bf16[4,256,3072]{2,1,0:T(8,128)(2,1)}) fusion(f32[4,256,3072]{2,1,0:T(8,128)} %fusion.79, f32[3072]{0:T(1024)S(1)} %convert_element_type.182, bf16[4,256,768]{2,1,0:T(8,128)(2,1)S(1)} %copy-done.15, bf16[3072,768]{1,0:T(8,128)(2,1)S(1)} %bitcast.200), kind=kOutput, calls=%fused_computation.23 | convolution fusion | flops 4904186880 | bytes 25190400 | tf_op jit(solution)/shard_map/rsd,fd->rsf/dot_general | solution.py:156
  312.2 8.5 %multiply_reduce_fusion.2 = (f32[768]{0:T(1024)}, f32[4,256]{1,0:T(4,128)S(1)}, f32[768]{0:T(1024)}, f32[4,256,768]{2,1,0:T(8,128)S(1)}) fusion(f32[4,256,768]{2,1,0:T(8,128)S(1)} %get-tuple-element.178, f32[4,256]{1,0:T(4,128)S(1)} %fusion.145, f32[4,256]{1,0:T(4,128)S(1)} %broadcast_multiply_fusion, f32[768]{0:T(1024)S(1)} %convert_element_type.179, ...), kind=kOutput, calls=%fused_computation.101 | convolution fusion | flops 4838126592 | bytes 17323008 | tf_op jit(solution)/shard_map/rsf,df->rsd/dot_general | solution.py:160
  324.7 4.1 bitcast_convert_fusion.3
  328.8 4.4 convolution_convert_fusion
  333.2 4.4 all-to-all-start.4
  337.6 12.5 %bitcast_convert_fusion = bf16[3072,768]{1,0:T(8,128)(2,1)} fusion(bf16[4,256,768]{2,1,0:T(8,128)(2,1)S(1)} %copy-done.15, f32[4,256,3072]{2,1,0:T(8,128)} %fusion.79, f32[3072]{0:T(1024)S(1)} %convert_element_type.182), kind=kOutput, calls=%fused_computation.45 | convolution fusion | flops 4865654784 | bytes 18886656 | tf_op jit(solution)/shard_map/rsf,rsd->fd/dot_general | solution.py:154
  350.9 23.1 %all-to-all-done.4 = bf16[24,256,128]{2,1,0:T(8,128)(2,1)} async-done(((bf16[24,256,128]{2,1,0:T(8,128)(2,1)}), bf16[24,256,128]{2,1,0:T(8,128)(2,1)}, u32[]{:S(2)}, u32[]{:S(2)}) %all-to-all-start.4) | async-done | bytes 1572896 | tf_op jit(solution)/shard_map/all_to_all | solution.py:173
  374.1 3.9 copy.123
  378.0 3.0 reshape.475
  380.9 8.8 %fusion.110 = f32[6,512,2,64]{1,3,2,0:T(8,128)} fusion(f32[6,2,512,512]{2,3,1,0:T(8,128)} %copy-done.9, f32[6,2,512]{2,1,0:T(2,128)S(1)} %log_add_fusion.1, pred[6,512,512]{1,2,0:T(8,128)(4,1)} %or_and_fusion.1, bf16[6,1024,2,64]{1,3,2,0:T(8,128)(2,1)S(1)} %reshape.475), kind=kOutput, calls=%fused_computation.130 | convolution fusion | flops 415236096 | bytes 16539648 | tf_op jit(solution)/shard_map/ihqk,iqhc->ikhc/dot_general | solution.py:211
  389.8 13.9 %fusion.95 = bf16[6,1024,2,64]{1,3,2,0:T(8,128)(2,1)} fusion(f32[6,512,2,64]{1,3,2,0:T(8,128)} %fusion.110, f32[6,2,512,1024]{3,2,1,0:T(8,128)} %get-tuple-element.174, f32[6,2,512]{2,1,0:T(2,128)S(1)} %log_add_fusion, pred[6,512,1024]{2,1,0:T(8,128)(4,1)S(1)} %copy-done.12, bf16[6,1024,2,64]{1,3,2,0:T(8,128)(2,1)S(1)} %reshape.475), kind=kOutput, calls=%fused_computation.97 | convolution fusion | flops 832045056 | bytes 32268288 | tf_op jit(solution)/shard_map/ihqk,iqhc->ikhc/dot_general | solution.py:211
  403.7 4.1 copy.134
  407.7 4.5 all-to-all-start.7
  412.3 10.8 %bitcast_convert_fusion.1 = bf16[768,3072]{1,0:T(8,128)(2,1)} fusion(bf16[4,256,3072]{2,1,0:T(8,128)(2,1)} %get-tuple-element.182, f32[4,256,768]{2,1,0:T(8,128)} %copy-done.10, f32[768]{0:T(1024)S(1)} %convert_element_type.180, f32[768]{0:T(1024)S(1)} %convert_element_type.179, f32[4,256]{1,0:T(4,128)S(1)} %fusion.145, f32[4,256]{1,0:T(4,128)S(1)} %broadcast_multiply_fusion), kind=kOutput, calls=%fused_computation.46 | convolution fusion | flops 4838129664 | bytes 14170112 | tf_op jit(solution)/shard_map/rsd,rsf->df/dot_general | solution.py:159
  424.5 7.5 fusion.129
  432.0 23.1 %fusion.113 = f32[6,512,2,64]{1,3,2,0:T(8,128)} fusion(f32[6,2,512,512]{2,3,1,0:T(8,128)} %fusion.129, f32[6,2,512,512]{2,3,1,0:T(8,128)} %copy-done.9, f32[6,2,512]{2,1,0:T(2,128)S(1)} %log_add_fusion.1, pred[6,512,512]{1,2,0:T(8,128)(4,1)} %or_and_fusion.1, bf16[6,1024,2,64]{1,3,2,0:T(8,128)(2,1)} %reshape.468), kind=kOutput, calls=%fused_computation.131 | convolution fusion | flops 437262848 | bytes 55885824 | tf_op jit(solution)/shard_map/ihqk,iqhc->ikhc/dot_general | solution.py:203
  455.1 11.5 %fusion.126 = f32[6,2,512,1024]{3,2,1,0:T(8,128)} fusion(bf16[6,1024,2,64]{1,3,2,0:T(8,128)(2,1)S(1)} %copy-done.8, bf16[6,1024,2,64]{1,3,2,0:T(8,128)(2,1)} %copy-done.14), kind=kOutput, calls=%fused_computation.140 | convolution fusion | flops 805306368 | bytes 27525120 | tf_op jit(solution)/shard_map/iqhc,ikhc->ihqk/dot_general | solution.py:192
  466.6 43.4 %fusion.96 = bf16[6,1024,2,64]{1,3,2,0:T(8,128)(2,1)S(1)} fusion(f32[6,512,2,64]{1,3,2,0:T(8,128)} %fusion.113, f32[6,2,512,1024]{3,2,1,0:T(8,128)} %fusion.126, f32[6,2,512,1024]{3,2,1,0:T(8,128)} %get-tuple-element.174, f32[6,2,512]{2,1,0:T(2,128)S(1)} %log_add_fusion, pred[6,512,1024]{2,1,0:T(8,128)(4,1)} %or_and_fusion, ...), kind=kOutput, calls=%fused_computation.99 | convolution fusion | flops 876092416 | bytes 110936064 | tf_op jit(solution)/shard_map/ihqk,iqhc->ikhc/dot_general | solution.py:203
  510.0 3.2 copy.130
  513.2 4.9 all-to-all-start.6
  518.1 20.1 %fusion.116 = bf16[6,2,64,512]{3,2,1,0:T(8,128)(2,1)} fusion(f32[6,2,512,512]{2,3,1,0:T(8,128)} %fusion.129, f32[6,2,512,512]{2,3,1,0:T(8,128)} %copy-done.9, f32[6,2,512]{2,1,0:T(2,128)S(1)} %log_add_fusion.1, pred[6,512,512]{1,2,0:T(8,128)(4,1)} %or_and_fusion.1, bf16[6,1024,2,64]{1,3,2,0:T(8,128)(2,1)} %reshape.470), kind=kOutput, calls=%fused_computation.132 | convolution fusion | flops 437656064 | bytes 55099392 | tf_op jit(solution)/shard_map/ihqk,ikhc->iqhc/dot_general | solution.py:198
  539.9 42.1 %fusion.119 = bf16[6,2,64,512]{3,2,1,0:T(8,128)(2,1)} fusion(bf16[6,1024,2,64]{1,3,2,0:T(8,128)(2,1)} %reshape.470, f32[6,2,512,1024]{3,2,1,0:T(8,128)} %fusion.126, f32[6,2,512,1024]{3,2,1,0:T(8,128)} %get-tuple-element.174, f32[6,2,512]{2,1,0:T(2,128)S(1)} %log_add_fusion, pred[6,512,1024]{2,1,0:T(8,128)(4,1)} %or_and_fusion), kind=kOutput, calls=%fused_computation.133 | convolution fusion | flops 874912768 | bytes 55861248 | tf_op jit(solution)/shard_map/ihqk,ikhc->iqhc/dot_general | solution.py:198
  587.4 5.1 all-to-all-start.5
  597.5 42.2 %all-to-all-done.5 = bf16[6,1024,128]{2,0,1:T(8,128)(2,1)} async-done(((bf16[6,1024,128]{2,0,1:T(8,128)(2,1)}), bf16[6,1024,128]{2,0,1:T(8,128)(2,1)}, u32[]{:S(2)}, u32[]{:S(2)}) %all-to-all-start.5) | async-done | bytes 1572896 | tf_op jit(solution)/shard_map/all_to_all | solution.py:223
  641.7 7.2 bitcast_convert_fusion.2
  648.9 4.7 copy.140
  653.8 13.5 %add_convert_fusion = bf16[4,256,768]{2,1,0:T(8,128)(2,1)} fusion(f32[4,256,768]{2,1,0:T(8,128)} %copy-done.10, bf16[3072,768]{1,0:T(8,128)(2,1)} %param.45, f32[768]{0:T(1024)S(1)} %convert_element_type.184, f32[4,256,3072]{2,1,0:T(8,128)} %fusion.79, f32[3072]{0:T(1024)S(1)} %convert_element_type.182), kind=kOutput, calls=%fused_computation.106 | convolution fusion | flops 4865654784 | bytes 22035456 | tf_op jit(solution)/shard_map/rsf,fd->rsd/dot_general | solution.py:150
  667.4 30.8 %reduce-scatter.5.cloned.1.call-done = bf16[96,1920]{1,0:T(8,128)(2,1)} async-done(((bf16[768,1920]{1,0:T(8,128)(2,1)}), bf16[96,1920]{1,0:T(8,128)(2,1)}) %reduce-scatter.5.cloned.1.call-update) | async-done | bytes 368656 | tf_op jit(solution)/shard_map/reduce_scatter | solution.py:264
  698.2 7.3 bitcast_reduce_fusion
  705.5 3.3 copy.138
  708.8 3.0 copy.144
  713.3 3.2 fusion.91
  716.6 4.3 convert_reduce_fusion.2
  720.9 20.5 %all-reduce.3 = (f32[768]{0:T(1024)S(1)}, f32[768]{0:T(1024)S(1)}, f32[768]{0:T(1024)S(1)}, f32[384]{0:T(512)S(1)}, f32[768]{0:T(1024)S(1)}, /*index=5*/f32[768]...) all-reduce(f32[768]{0:T(1024)S(1)} %get-tuple-element.130, ...), channel_id=1, replica_groups=mesh['seq'=8,'head'=4] {'head'}, use_global_device_ids=true, to_apply=%region_17.18 | all-reduce | flops 8832 | bytes 70656 | tf_op jit(solution)/shard_map/psum | solution.py:247
  741.4 24.5 %all-reduce.2 = (f32[768]{0:T(1024)}, f32[768]{0:T(1024)}, f32[768]{0:T(1024)}, f32[384]{0:T(512)}, f32[768]{0:T(1024)}, /*index=5*/f32[768]{0:T(1024)}, f32[768]{0:T(1024)}, f32[3072]{0:T(1024)}, f32[768]{0:T(1024)}) all-reduce(f32[768]{0:T(1024)S(1)} %get-tuple-element.146, ...), channel_id=1, replica_groups=mesh['seq'=8,'head'=4] {'seq'}, use_global_device_ids=true, to_apply=%region_18.19 | all-reduce | flops 8832 | bytes 70656 | tf_op jit(solution)/shard_map/psum | solution.py:246
  766.0 10.8 %all-reduce.7.cloned.1.call-done = (bf16[96,1920]{1,0:T(8,128)(2,1)}, bf16[96,768]{1,0:T(8,128)(2,1)}, bf16[96,3072]{1,0:T(8,128)(2,1)}, bf16[384,768]{1,0:T(8,128)(2,1)}) async-done(((bf16[96,1920]{1,0:T(8,128)(2,1)}, bf16[96,768]{1,0:T(8,128)(2,1)}, bf16[96,3072]{1,0:T(8,128)(2,1)}, bf16[384,768]{1,0:T(8,128)(2,1)}), (bf16[96,1920]{1,0:T(8,128)(2,1)}, bf16[96,768]{1,0:T(8,128)(2,1)}, ...) | async-done | bytes 1695760 | tf_op jit(solution)/shard_map/psum | solution.py:278
  (188 shorter events, 53.7 us)
Async XLA Ops:
  7.2 277.4 %copy-start = (bf16[768,768]{1,0:T(8,128)(2,1)S(1)}, bf16[768,768]{1,0:T(8,128)(2,1)}, u32[]{:S(2)}) copy-start(bf16[768,768]{1,0:T(8,128)(2,1)} %param.39) | copy-start | bytes 3538948
  7.2 6.5 copy-start.21
  8.7 10.6 %copy-start.33 = (f32[768]{0:T(1024)}, f32[768]{0:T(1024)S(1)}, u32[]{:S(2)}) copy-start(f32[768]{0:T(1024)S(1)} %convert_element_type.166) | copy-start | bytes 9220
  11.7 7.7 copy-start.31
  13.7 5.6 copy-start.35
  14.7 4.7 copy-start.4
  24.8 3.1 copy-start.18
  28.0 7.6 copy-start.49
  29.3 43.4 %all-to-all-start = ((bf16[24,256,128]{2,1,0:T(8,128)(2,1)}), bf16[24,256,128]{2,1,0:T(8,128)(2,1)}, u32[]{:S(2)}, u32[]{:S(2)}) async-start(bf16[24,256,128]{2,1,0:T(8,128)(2,1)} %bitcast.172), calls=%async_computation | async-start | bytes 3145728 | tf_op jit(solution)/shard_map/all_to_all | solution.py:89
  72.7 7.8 copy-start.44
  72.7 46.3 %copy-start.45 = (s32[4,256]{1,0:T(4,128)S(1)}, s32[4,256]{1,0:T(4,128)}, u32[]{:S(2)}) copy-start(s32[4,256]{1,0:T(4,128)} %param.33) | copy-start | bytes 12292
  72.7 59.8 %all-to-all-start.1 = ((bf16[24,256,128]{2,1,0:T(8,128)(2,1)}), bf16[24,256,128]{2,1,0:T(8,128)(2,1)}, u32[]{:S(2)}, u32[]{:S(2)}) async-start(bf16[24,256,128]{2,1,0:T(8,128)(2,1)} %bitcast.178), calls=%async_computation.1 | async-start | bytes 3145728 | tf_op jit(solution)/shard_map/all_to_all | solution.py:83
  132.5 35.6 %all-to-all-start.2 = ((bf16[24,256,128]{2,1,0:T(8,128)(2,1)}), bf16[24,256,128]{2,1,0:T(8,128)(2,1)}, u32[]{:S(2)}, u32[]{:S(2)}) async-start(bf16[24,256,128]{2,1,0:T(8,128)(2,1)} %bitcast.171), calls=%async_computation.2 | async-start | bytes 3145728 | tf_op jit(solution)/shard_map/all_to_all | solution.py:86
  175.6 4.8 copy-start.17
  180.4 4.7 copy-start.9
  180.4 4.7 copy-start.23
  180.4 4.7 copy-start.6
  185.1 4.2 copy-start.25
  190.8 13.5 %copy-start.11 = (pred[6,512,1024]{2,1,0:T(8,128)(4,1)S(1)}, pred[6,512,1024]{2,1,0:T(8,128)(4,1)}, u32[]{:S(2)}) copy-start(pred[6,512,1024]{2,1,0:T(8,128)(4,1)} %or_and_fusion) | copy-start | bytes 9437188
  204.3 11.9 %copy-start.27 = (f32[6,2,512]{2,1,0:T(2,128)}, f32[6,2,512]{2,1,0:T(2,128)S(1)}, u32[]{:S(2)}) copy-start(f32[6,2,512]{2,1,0:T(2,128)S(1)} %get-tuple-element.173) | copy-start | bytes 73732
  204.3 11.9 %copy-start.7 = (bf16[6,1024,2,64]{1,3,2,0:T(8,128)(2,1)S(1)}, bf16[6,1024,2,64]{1,3,2,0:T(8,128)(2,1)}, u32[]{:S(2)}) copy-start(bf16[6,1024,2,64]{1,3,2,0:T(8,128)(2,1)} %reshape.466) | copy-start | bytes 4718596
  216.2 11.5 %copy-start.29 = (f32[6,2,512]{2,1,0:T(2,128)}, f32[6,2,512]{2,1,0:T(2,128)S(1)}, u32[]{:S(2)}) copy-start(f32[6,2,512]{2,1,0:T(2,128)S(1)} %fusion.3) | copy-start | bytes 73732
  232.5 4.7 copy-start.50
  232.5 4.7 copy-start.51
  232.5 4.7 copy-start.52
  232.5 4.7 copy-start.43
  232.5 50.2 %all-to-all-start.3 = ((bf16[6,1024,128]{2,0,1:T(8,128)(2,1)}), bf16[6,1024,128]{2,0,1:T(8,128)(2,1)}, u32[]{:S(2)}, u32[]{:S(2)}) async-start(bf16[6,1024,128]{2,0,1:T(8,128)(2,1)} %pad_maximum_fusion.1), calls=%async_computation.3 | async-start | bytes 4194304 | tf_op jit(solution)/shard_map/all_to_all | solution.py:131
  237.1 430.2 %reduce-scatter.7.cloned.1.call-start = ((), (), s32[]{:S(2)}) async-start(), calls=%async_computation.13 | async-start | bytes 1327104 | tf_op jit(solution)/shard_map/reduce_scatter | solution.py:267
  284.6 2.2 slice-start
  284.6 2.3 slice-start.1
  284.6 10.8 %slice-start.2 = ((s8[4718592]{0:T(1024)(128)(4,1)}), s8[4194304]{0:T(1024)(128)(4,1)S(1)}, s32[]{:S(2)}) async-start(s8[4718592]{0:T(1024)(128)(4,1)} %bitcast.199), calls=%async_computation.19 | async-start | bytes 8388608
  286.2 34.5 %copy-start.10 = (f32[4,256,768]{2,1,0:T(8,128)}, f32[4,256,768]{2,1,0:T(8,128)S(1)}, u32[]{:S(2)}) copy-start(f32[4,256,768]{2,1,0:T(8,128)S(1)} %get-tuple-element.178) | copy-start | bytes 9437188
  286.9 8.5 %copy-start.15 = (bf16[4,256,768]{2,1,0:T(8,128)(2,1)S(1)}, bf16[4,256,768]{2,1,0:T(8,128)(2,1)}, u32[]{:S(2)}) copy-start(bf16[4,256,768]{2,1,0:T(8,128)(2,1)} %param.47) | copy-start | bytes 4718596
  286.9 8.5 %slice-start.3 = ((s8[4718592]{0:T(1024)(128)(4,1)}), s8[524288]{0:T(1024)(128)(4,1)S(1)}, s32[]{:S(2)}) async-start(s8[4718592]{0:T(1024)(128)(4,1)} %bitcast.199), calls=%async_computation.20 | async-start | bytes 1048576
  321.9 1.7 copy-start.2
  321.9 1.6 copy-start.37
  333.2 40.9 %all-to-all-start.4 = ((bf16[24,256,128]{2,1,0:T(8,128)(2,1)}), bf16[24,256,128]{2,1,0:T(8,128)(2,1)}, u32[]{:S(2)}, u32[]{:S(2)}) async-start(bf16[24,256,128]{2,1,0:T(8,128)(2,1)} %bitcast.189), calls=%async_computation.4 | async-start | bytes 3145728 | tf_op jit(solution)/shard_map/all_to_all | solution.py:173
  337.5 329.8 %reduce-scatter.11.cloned.1.call-start = ((), (), s32[]{:S(2)}) async-start(), calls=%async_computation.15 | async-start | bytes 5308416 | tf_op jit(solution)/shard_map/reduce_scatter | solution.py:273
  380.9 8.8 %copy-start.14 = (bf16[6,1024,2,64]{1,3,2,0:T(8,128)(2,1)}, bf16[6,1024,2,64]{1,3,2,0:T(8,128)(2,1)S(1)}, u32[]{:S(2)}) copy-start(bf16[6,1024,2,64]{1,3,2,0:T(8,128)(2,1)S(1)} %reshape.475) | copy-start | bytes 4718596
  380.9 8.8 %copy-start.12 = (pred[6,512,1024]{2,1,0:T(8,128)(4,1)S(1)}, pred[6,512,1024]{2,1,0:T(8,128)(4,1)}, u32[]{:S(2)}) copy-start(pred[6,512,1024]{2,1,0:T(8,128)(4,1)} %or_and_fusion) | copy-start | bytes 9437188
  407.7 105.5 %all-to-all-start.7 = ((bf16[6,1024,128]{2,0,1:T(8,128)(2,1)}), bf16[6,1024,128]{2,0,1:T(8,128)(2,1)}, u32[]{:S(2)}, u32[]{:S(2)}) async-start(bf16[6,1024,128]{2,0,1:T(8,128)(2,1)} %copy.134), calls=%async_computation.7 | async-start | bytes 4194304 | tf_op jit(solution)/shard_map/all_to_all | solution.py:225
  412.2 255.2 %reduce-scatter.9.cloned.1.call-start = ((), (), s32[]{:S(2)}) async-start(), calls=%async_computation.14 | async-start | bytes 5308416 | tf_op jit(solution)/shard_map/reduce_scatter | solution.py:270
  513.2 74.2 %all-to-all-start.6 = ((bf16[6,1024,128]{2,0,1:T(8,128)(2,1)}), bf16[6,1024,128]{2,0,1:T(8,128)(2,1)S(1)}, u32[]{:S(2)}, u32[]{:S(2)}) async-start(bf16[6,1024,128]{2,0,1:T(8,128)(2,1)} %copy.130), calls=%async_computation.6 | async-start | bytes 4194304 | tf_op jit(solution)/shard_map/all_to_all | solution.py:224
  587.4 52.3 %all-to-all-start.5 = ((bf16[6,1024,128]{2,0,1:T(8,128)(2,1)}), bf16[6,1024,128]{2,0,1:T(8,128)(2,1)}, u32[]{:S(2)}, u32[]{:S(2)}) async-start(bf16[6,1024,128]{2,0,1:T(8,128)(2,1)} %pad_maximum_fusion.2), calls=%async_computation.5 | async-start | bytes 4194304 | tf_op jit(solution)/shard_map/all_to_all | solution.py:223
  592.5 105.7 %reduce-scatter.5.cloned.1.call-start = ((), (), s32[]{:S(2)}) async-start(), calls=%async_computation.12 | async-start | bytes 3317760 | tf_op jit(solution)/shard_map/reduce_scatter | solution.py:264
  594.4 1.7 copy-start.13
  596.1 45.6 %copy-start.5 = (bf16[4,256,768]{2,1,0:T(8,128)(2,1)S(1)}, bf16[4,256,768]{2,1,0:T(8,128)(2,1)}, u32[]{:S(2)}) copy-start(bf16[4,256,768]{2,1,0:T(8,128)(2,1)} %param.30) | copy-start | bytes 4718596
  596.1 45.6 %copy-start.32 = (f32[4,256]{1,0:T(4,128)S(1)}, f32[4,256]{1,0:T(4,128)}, u32[]{:S(2)}) copy-start(f32[4,256]{1,0:T(4,128)} %copy-done.31) | copy-start | bytes 12292
  596.1 45.6 %copy-start.34 = (f32[768]{0:T(1024)S(1)}, f32[768]{0:T(1024)}, u32[]{:S(2)}) copy-start(f32[768]{0:T(1024)} %copy-done.33) | copy-start | bytes 9220
  596.1 45.6 %copy-start.36 = (f32[4,256]{1,0:T(4,128)S(1)}, f32[4,256]{1,0:T(4,128)}, u32[]{:S(2)}) copy-start(f32[4,256]{1,0:T(4,128)} %copy-done.35) | copy-start | bytes 12292
  596.1 45.6 %copy-start.46 = (f32[768]{0:T(1024)S(1)}, f32[768]{0:T(1024)}, u32[]{:S(2)}) copy-start(f32[768]{0:T(1024)} %convert_element_type.167) | copy-start | bytes 9220
  641.7 7.2 copy-start.19
  648.9 4.9 copy-start.53
  653.6 123.1 %all-reduce.7.cloned.1.call-start = ((), (), s32[]{:S(2)}) async-start(), calls=%async_computation.16 | async-start | bytes 3391488 | tf_op jit(solution)/shard_map/psum | solution.py:278
  705.5 7.8 copy-start.40
  711.8 4.7 copy-start.3
  711.8 4.7 copy-start.16
  711.8 4.7 copy-start.38
  716.5 4.3 copy-start.41
  716.5 4.3 copy-start.42
  716.6 4.3 copy-start.47
  716.6 4.3 copy-start.48
  716.6 67.0 %copy-start.1 = (bf16[768,768]{1,0:T(8,128)(2,1)S(1)}, bf16[768,768]{1,0:T(8,128)(2,1)}, u32[]{:S(2)}) copy-start(bf16[768,768]{1,0:T(8,128)(2,1)} %param.39) | copy-start | bytes 3538948
  776.7 5.8 copy-start.22
  (7 other events, 6.2 us)
Sparse Core Ops, SparseCore 0:
  328.9 35.8 reduce-scatter.6
  368.7 53.8 reduce-scatter.10
  426.1 53.8 reduce-scatter.8
  653.7 44.4 reduce-scatter.4
  700.8 75.8 all-reduce.6
